TPU v7x, 512 devices: a whole 4x4x16 slice. The times are simulated.
512 devices in a mesh: grp: 8 (over x, core), own: 64 (over z, y).
Axes of the slice: x: 4, y: 4, z: 16, core: 2. Of those that a mesh axis runs over, the one named last changes fastest.
Arguments:
- left: bfloat16 [32768, 128, 64], P(('grp', 'own')), may hold values from -0.75 to 0.75
- right: bfloat16 [32768, 128, 64], P(('grp', 'own')), may hold values from -0.75 to 0.75
- values: bfloat16 [32768, 128], P(('grp', 'own')), may hold values from -6 to 6
- core: bfloat16 [10240, 64, 64], P(('grp', 'own')), may hold values from -6 to 6
- tile_slice: int32 [32768], P(('grp', 'own')), may hold values from 0 to 10239, as said below
- tile_fill: int32 [32768], P(('grp', 'own')), may hold values from 64 to 128
Outputs:
- new_core: bfloat16 [10240, 64, 64], P(('grp', 'own'))
- new_left: bfloat16 [32768, 128, 64], P(('grp', 'own'))
Inputs may be any that keep to these rules, and one draw needn't show every extreme that they name: `tile_slice`: call j // 20 the block of slice j and its remainder mod 64 its class. Among the tiles of one device at most 2 have slices of one class; in every group of 64 consecutive devices some class gets exactly 2 tiles from every device of the group.
All inputs are finite; a program needn't handle non-finite values.
Results may differ from a plain program's by a relative error of at most 0.0052.
Values may be sent and summed in bfloat16 or wider, within the bound.
No kernel may reach another device: no remote copies, remote signals or barrier semaphores. Data moves between devices by JAX's collectives and lax.ppermute only.
A program may use at most 64 MiB of HBM per device.

v0:
```python
import jax
import jax.numpy as jnp
from jax import lax
from jax.sharding import PartitionSpec as P


def tile_terms(left_tiles, right_tiles, value_tiles, fill_counts, slice_tables):
    tile_rows = left_tiles.shape[1]
    projected = jnp.einsum(
        "sea,sab->seb", left_tiles, slice_tables, preferred_element_type=jnp.float32
    )
    predicted = jnp.sum(projected * right_tiles.astype(jnp.float32), axis=-1)
    live_rows = jnp.arange(tile_rows)[None, :] < fill_counts[:, None]
    residual = jnp.where(live_rows, predicted - value_tiles.astype(jnp.float32), 0.0)
    weighted = (residual[:, :, None] * left_tiles.astype(jnp.float32)).astype(jnp.bfloat16)
    return jnp.einsum("sea,seb->sab", weighted, right_tiles, preferred_element_type=jnp.float32)


def body(left, right, values, core, tile_slice, tile_fill):
    owners = lax.axis_size("own")
    groups = lax.axis_size("grp")
    tile_count, tile_rows, rank_width = left.shape
    per_device = core.shape[0]
    local_count = groups * per_device
    slot_cap = 2 * tile_count // owners
    slot_total = owners * slot_cap
    dev_block = tile_slice // per_device
    target_owner = dev_block % owners
    local_slice = dev_block // owners * per_device + tile_slice % per_device
    positions = jnp.arange(tile_count)
    same_owner = target_owner[:, None] == target_owner[None, :]
    earlier = positions[None, :] < positions[:, None]
    rank_among = jnp.sum((same_owner & earlier).astype(jnp.int32), axis=1)
    slot_of_tile = target_owner * slot_cap + rank_among
    slot_match = slot_of_tile[None, :] == jnp.arange(slot_total)[:, None]
    slot_live = jnp.any(slot_match, axis=1)
    tile_of_slot = jnp.sum(jnp.where(slot_match, positions[None, :], 0), axis=1)
    send_slice = jnp.where(slot_live, local_slice[tile_of_slot], 0)
    old_tables = lax.all_gather(core, "grp", axis=0, tiled=True)
    send_left = left[tile_of_slot]
    send_right = right[tile_of_slot]
    send_values = values[tile_of_slot]
    send_fill = jnp.where(slot_live, tile_fill[tile_of_slot], 0)
    got_left, got_right, got_values, got_slice, got_fill = (
        lax.all_to_all(send_left, "own", split_axis=0, concat_axis=0, tiled=True),
        lax.all_to_all(send_right, "own", split_axis=0, concat_axis=0, tiled=True),
        lax.all_to_all(send_values, "own", split_axis=0, concat_axis=0, tiled=True),
        lax.all_to_all(send_slice, "own", split_axis=0, concat_axis=0, tiled=True),
        lax.all_to_all(send_fill, "own", split_axis=0, concat_axis=0, tiled=True),
    )
    tile_grad = tile_terms(got_left, got_right, got_values, got_fill, old_tables[got_slice])
    selector = (got_slice[:, None] == jnp.arange(local_count)[None, :]).astype(jnp.float32)
    grad_part = jnp.dot(
        selector.T,
        tile_grad.reshape(slot_total, rank_width * rank_width),
        precision=lax.Precision.HIGHEST,
        preferred_element_type=jnp.float32,
    ).reshape(local_count, rank_width, rank_width)
    grad_whole = lax.psum(grad_part, "grp")
    new_tables = (old_tables.astype(jnp.float32) - grad_whole).astype(jnp.bfloat16)
    new_mine = lax.dynamic_slice_in_dim(
        new_tables, lax.axis_index("grp") * per_device, per_device, 0
    )
    refreshed = jnp.einsum(
        "sea,sab->seb", got_left, new_tables[got_slice], preferred_element_type=jnp.float32
    ).astype(jnp.bfloat16)
    returned = lax.all_to_all(refreshed, "own", split_axis=0, concat_axis=0, tiled=True)
    new_left = returned[slot_of_tile]
    return (new_mine, new_left)


def solution(mesh):
    return jax.shard_map(
        body,
        mesh=mesh,
        in_specs=(
            P(("grp", "own"), None, None),
            P(("grp", "own"), None, None),
            P(("grp", "own"), None),
            P(("grp", "own"), None, None),
            P(("grp", "own")),
            P(("grp", "own")),
        ),
        out_specs=(P(("grp", "own"), None, None), P(("grp", "own"), None, None)),
        check_vma=False,
    )
```

profile of v0, /device:TPU:7, one launch (start us, length us, event | category | flops | bytes accessed | tf_op | source)
XLA Modules:
  0.0 528.3 jit_solution(8652673713095691326)
XLA Ops:
  12.0 18.5 %all-to-all-start.1 = ((s32[64,2,1]{1,2,0:T(1,128)}), s32[64,2,1]{1,2,0:T(1,128)S(1)}, u32[]{:S(2)}, u32[]{:S(2)}) async-start(s32[64,2,1]{1,2,0:T(1,128)} %bitcast.4), calls=%async_computation.1 | async-start | bytes 65536 | tf_op jit(solution)/shard_map/all_to_all | solution.py:49
  31.2 12.7 %all-to-all-done.1 = s32[64,2,1]{1,2,0:T(1,128)S(1)} async-done(((s32[64,2,1]{1,2,0:T(1,128)}), s32[64,2,1]{1,2,0:T(1,128)S(1)}, u32[]{:S(2)}, u32[]{:S(2)}) %all-to-all-start.1) | async-done | bytes 544 | tf_op jit(solution)/shard_map/all_to_all | solution.py:49
  43.8 4.6 all-to-all-start
  50.6 11.4 %all-to-all-done = s32[64,2,1]{1,2,0:T(1,128)S(1)} async-done(((s32[64,2,1]{1,2,0:T(1,128)}), s32[64,2,1]{1,2,0:T(1,128)S(1)}, u32[]{:S(2)}, u32[]{:S(2)}) %all-to-all-start) | async-done | bytes 544 | tf_op jit(solution)/shard_map/all_to_all | solution.py:48
  61.9 4.7 all-to-all-start.3
  66.6 3.4 gather_fusion.2
  70.0 90.1 %all-to-all-done.3 = bf16[128,128,64]{1,2,0:T(8,128)(2,1)S(1)} async-done(((bf16[128,128,64]{1,2,0:T(8,128)(2,1)}), bf16[128,128,64]{1,2,0:T(8,128)(2,1)S(1)}, u32[]{:S(2)}, u32[]{:S(2)}) %all-to-all-start.3) | async-done | bytes 2097184 | tf_op jit(solution)/shard_map/all_to_all | solution.py:46
  161.5 10.7 %all-to-all-start.2 = ((bf16[128,128,64]{1,2,0:T(8,128)(2,1)}), bf16[128,128,64]{1,2,0:T(8,128)(2,1)S(1)}, u32[]{:S(2)}, u32[]{:S(2)}) async-start(bf16[128,128,64]{1,2,0:T(8,128)(2,1)} %gather_fusion.2), calls=%async_computation.2 | async-start | bytes 4194304 | tf_op jit(solution)/shard_map/all_to_all | solution.py:45
  176.7 34.6 %all-gather.2.cloned.1.call-done = bf16[160,64,64]{2,1,0:T(8,128)(2,1)} async-done(((bf16[20,64,64]{2,1,0:T(8,128)(2,1)}), bf16[160,64,64]{2,1,0:T(8,128)(2,1)}) %all-gather.2.cloned.1.call-update) | async-done | bytes 1310736 | tf_op jit(solution)/shard_map/all_gather | solution.py:39
  211.3 3.9 gather_fusion.3
  215.2 50.7 %all-to-all-done.2 = bf16[128,128,64]{1,2,0:T(8,128)(2,1)S(1)} async-done(((bf16[128,128,64]{1,2,0:T(8,128)(2,1)}), bf16[128,128,64]{1,2,0:T(8,128)(2,1)S(1)}, u32[]{:S(2)}, u32[]{:S(2)}) %all-to-all-start.2) | async-done | bytes 2097184 | tf_op jit(solution)/shard_map/all_to_all | solution.py:45
  265.9 11.0 %all-to-all-start.4 = ((bf16[64,2,128]{2,1,0:T(2,128)(2,1)}), bf16[64,2,128]{2,1,0:T(2,128)(2,1)S(1)}, u32[]{:S(2)}, u32[]{:S(2)}) async-start(bf16[64,2,128]{2,1,0:T(2,128)(2,1)} %bitcast.6), calls=%async_computation.4 | async-start | bytes 65536 | tf_op jit(solution)/shard_map/all_to_all | solution.py:47
  280.4 9.9 %all-to-all-done.4 = bf16[64,2,128]{2,1,0:T(2,128)(2,1)S(1)} async-done(((bf16[64,2,128]{2,1,0:T(2,128)(2,1)}), bf16[64,2,128]{2,1,0:T(2,128)(2,1)S(1)}, u32[]{:S(2)}, u32[]{:S(2)}) %all-to-all-start.4) | async-done | bytes 32800 | tf_op jit(solution)/shard_map/all_to_all | solution.py:47
  290.4 4.8 fusion
  295.2 4.8 copy.30
  299.9 5.4 %fusion.1 = f32[160,64,64]{0,2,1:T(8,128)} fusion(f32[128,64,64]{0,2,1:T(8,128)} %copy.30, s32[128]{0:T(128)S(1)} %eq.50), kind=kOutput, calls=%fused_computation.12 | convolution fusion | flops 1006653440 | bytes 4719104 | tf_op jit(solution)/shard_map/dot_general | solution.py:53
  305.3 4.9 copy.26
  310.3 75.1 %all-reduce.2.cloned.1.call-done = f32[160,64,64]{0,2,1:T(8,128)} async-done(((f32[160,64,64]{0,2,1:T(8,128)}), f32[160,64,64]{0,2,1:T(8,128)}) %all-reduce.2.cloned.1.call-update) | async-done | bytes 2621456 | tf_op jit(solution)/shard_map/psum | solution.py:59
  385.4 5.0 subtract_convert_fusion
  390.4 5.0 copy.31
  395.4 3.9 gather_fusion.6
  399.3 3.8 convolution_convert_fusion
  403.0 15.8 %all-to-all-start.5 = ((bf16[128,128,64]{1,2,0:T(8,128)(2,1)}), bf16[128,128,64]{1,2,0:T(8,128)(2,1)}, u32[]{:S(2)}, u32[]{:S(2)}) async-start(bf16[128,128,64]{1,2,0:T(8,128)(2,1)} %convolution_convert_fusion), calls=%async_computation.5 | async-start | bytes 4194304 | tf_op jit(solution)/shard_map/all_to_all | solution.py:67
  422.8 95.4 %all-to-all-done.5 = bf16[128,128,64]{1,2,0:T(8,128)(2,1)} async-done(((bf16[128,128,64]{1,2,0:T(8,128)(2,1)}), bf16[128,128,64]{1,2,0:T(8,128)(2,1)}, u32[]{:S(2)}, u32[]{:S(2)}) %all-to-all-start.5) | async-done | bytes 2097184 | tf_op jit(solution)/shard_map/all_to_all | solution.py:67
  (41 shorter events, 24.2 us)
Async XLA Ops:
  7.2 41.3 %copy-start = (bf16[64,128,64]{1,2,0:T(8,128)(2,1)S(1)}, bf16[64,128,64]{1,2,0:T(8,128)(2,1)}, u32[]{:S(2)}) copy-start(bf16[64,128,64]{1,2,0:T(8,128)(2,1)} %param.7) | copy-start | bytes 3145732
  12.0 31.9 %all-to-all-start.1 = ((s32[64,2,1]{1,2,0:T(1,128)}), s32[64,2,1]{1,2,0:T(1,128)S(1)}, u32[]{:S(2)}, u32[]{:S(2)}) async-start(s32[64,2,1]{1,2,0:T(1,128)} %bitcast.4), calls=%async_computation.1 | async-start | bytes 65536 | tf_op jit(solution)/shard_map/all_to_all | solution.py:49
  43.8 18.1 %all-to-all-start = ((s32[64,2,1]{1,2,0:T(1,128)}), s32[64,2,1]{1,2,0:T(1,128)S(1)}, u32[]{:S(2)}, u32[]{:S(2)}) async-start(s32[64,2,1]{1,2,0:T(1,128)} %bitcast.2), calls=%async_computation | async-start | bytes 65536 | tf_op jit(solution)/shard_map/all_to_all | solution.py:48
  61.9 98.2 %all-to-all-start.3 = ((bf16[128,128,64]{1,2,0:T(8,128)(2,1)}), bf16[128,128,64]{1,2,0:T(8,128)(2,1)S(1)}, u32[]{:S(2)}, u32[]{:S(2)}) async-start(bf16[128,128,64]{1,2,0:T(8,128)(2,1)} %gather_fusion.4), calls=%async_computation.3 | async-start | bytes 4194304 | tf_op jit(solution)/shard_map/all_to_all | solution.py:46
  70.0 102.9 %copy-start.3 = (bf16[64,128]{1,0:T(8,128)(2,1)S(1)}, bf16[64,128]{1,0:T(8,128)(2,1)}, u32[]{:S(2)}) copy-start(bf16[64,128]{1,0:T(8,128)(2,1)} %param.8) | copy-start | bytes 49156
  160.2 1.3 copy-start.1
  161.5 104.4 %all-to-all-start.2 = ((bf16[128,128,64]{1,2,0:T(8,128)(2,1)}), bf16[128,128,64]{1,2,0:T(8,128)(2,1)S(1)}, u32[]{:S(2)}, u32[]{:S(2)}) async-start(bf16[128,128,64]{1,2,0:T(8,128)(2,1)} %gather_fusion.2), calls=%async_computation.2 | async-start | bytes 4194304 | tf_op jit(solution)/shard_map/all_to_all | solution.py:45
  172.2 39.1 %all-gather.2.cloned.1.call-start = ((), (), s32[]{:S(2)}) async-start(), calls=%async_computation.6 | async-start | bytes 2949120 | tf_op jit(solution)/shard_map/all_gather | solution.py:39
  265.9 24.4 %all-to-all-start.4 = ((bf16[64,2,128]{2,1,0:T(2,128)(2,1)}), bf16[64,2,128]{2,1,0:T(2,128)(2,1)S(1)}, u32[]{:S(2)}, u32[]{:S(2)}) async-start(bf16[64,2,128]{2,1,0:T(2,128)(2,1)} %bitcast.6), calls=%async_computation.4 | async-start | bytes 65536 | tf_op jit(solution)/shard_map/all_to_all | solution.py:47
  276.9 108.5 %all-reduce.2.cloned.1.call-start = ((), (), s32[]{:S(2)}) async-start(), calls=%async_computation.7 | async-start | bytes 8388608 | tf_op jit(solution)/shard_map/psum | solution.py:59
  403.0 15.8 %copy-start.2 = (bf16[160,64,64]{0,2,1:T(8,128)(2,1)S(1)}, bf16[160,64,64]{0,2,1:T(8,128)(2,1)}, u32[]{:S(2)}) copy-start(bf16[160,64,64]{0,2,1:T(8,128)(2,1)} %subtract_convert_fusion) | copy-start | bytes 3932164
  403.0 115.2 %all-to-all-start.5 = ((bf16[128,128,64]{1,2,0:T(8,128)(2,1)}), bf16[128,128,64]{1,2,0:T(8,128)(2,1)}, u32[]{:S(2)}, u32[]{:S(2)}) async-start(bf16[128,128,64]{1,2,0:T(8,128)(2,1)} %convolution_convert_fusion), calls=%async_computation.5 | async-start | bytes 4194304 | tf_op jit(solution)/shard_map/all_to_all | solution.py:67
Sparse Core Ops, SparseCore 0:
  175.1 36.1 all-gather.1
  305.5 79.8 all-reduce.1
where the time goes:
time: 529 us; the launch traced here: 528 us
  waiting for transfers between devices  381 us (72%)
  starting transfers between devices  65.5 us (12%)
  local copies, waits for them, and re-layouts  43.1 us (8%)
  matrix products  17.1 us (3%)
  between operations  14.2 us (3%)
  other arithmetic  7.74 us (1%)
    all_to_all x1, waiting for transfers between devices, body(): lax.all_to_all(refreshed, 'own', split_axis=0, concat_axis=0, tiled=True)  95.4 us
    all_to_all x1, waiting for transfers between devices, body(): lax.all_to_all(send_right, 'own', split_axis=0, concat_axis=0, tiled=True)  90.1 us
    psum x1, waiting for transfers between devices, body(): grad_whole = lax.psum(grad_part, 'grp')  75.1 us
    all_to_all x1, waiting for transfers between devices, body(): lax.all_to_all(send_left, 'own', split_axis=0, concat_axis=0, tiled=True)  50.7 us
    all_gather x1, waiting for transfers between devices, body(): old_tables = lax.all_gather(core, 'grp', axis=0, tiled=True)  34.6 us
    all_to_all x1, starting transfers between devices, body(): lax.all_to_all(send_fill, 'own', split_axis=0, concat_axis=0, tiled=True)  18.5 us
    all_to_all x1, starting transfers between devices, body(): lax.all_to_all(refreshed, 'own', split_axis=0, concat_axis=0, tiled=True)  15.8 us
    all_to_all x1, waiting for transfers between devices, body(): lax.all_to_all(send_fill, 'own', split_axis=0, concat_axis=0, tiled=True)  12.7 us
  transfers between devices with their start and end apart: 8, of which 8 were waited for; matrix products, arithmetic and copies ran while one was open for 5% of the time, Pallas kernels for 0%

commit v1 on v0

--- a/solution.py
+++ b/solution.py
@@ -2,6 +2,16 @@
 import jax.numpy as jnp
 from jax import lax
 from jax.sharding import PartitionSpec as P
+from jax.lax import axis_size, ppermute
+
+
+def _close_flows(z_in, ax_name):
+    world = axis_size(ax_name)
+    next_value = lambda big: [(dev_j, dev_j ^ big) for dev_j in range(world)]
+    view_out = z_in
+    for w in range(world.bit_length() - 1):
+        view_out = view_out + ppermute(view_out, axis_name=ax_name, perm=next_value(1 << w))
+    return view_out
 
 
 def tile_terms(left_tiles, right_tiles, value_tiles, fill_counts, slice_tables):
@@ -56,7 +66,7 @@
         precision=lax.Precision.HIGHEST,
         preferred_element_type=jnp.float32,
     ).reshape(local_count, rank_width, rank_width)
-    grad_whole = lax.psum(grad_part, "grp")
+    grad_whole = _close_flows(grad_part, "grp")
     new_tables = (old_tables.astype(jnp.float32) - grad_whole).astype(jnp.bfloat16)
     new_mine = lax.dynamic_slice_in_dim(
         new_tables, lax.axis_index("grp") * per_device, per_device, 0

time: 529 us -> 644 us (1.22)
  waiting for transfers between devices: 381 us -> 485 us
    ppermute x0 -> x3, waiting for transfers between devices: none -> 185 us  [_close_flows(): ppermute(view_out, axis_name=ax_name, perm=next_value(1 << w))]
    psum x1 -> x0, waiting for transfers between devices: 75.1 us -> none  [body(): grad_whole = lax.psum(grad_part, 'grp')]
    ppermute x0 -> x3, starting transfers between devices: none -> 10.9 us  [_close_flows(): ppermute(view_out, axis_name=ax_name, perm=next_value(1 << w))]
    all_to_all x1, starting transfers between devices: 15.8 us -> 5.69 us  [body(): lax.all_to_all(refreshed, 'own', split_axis=0, concat_axis=0, tiled=True)]
  transfers between devices with their start and end apart: 8 -> 10, of which waited for: 8 -> 10; matrix products, arithmetic and copies ran while one was open for 5% -> 4% of each run, Pallas kernels for 0% -> 0%
where the time goes in v1:
time: 644 us; the launch traced here: 637 us
  waiting for transfers between devices  485 us (75%)
  starting transfers between devices  66.2 us (10%)
  local copies, waits for them, and re-layouts  43.2 us (7%)
  matrix products  15.3 us (2%)
  between operations  14.3 us (2%)
  other arithmetic  13.3 us (2%)
    ppermute x3, waiting for transfers between devices, _close_flows(): ppermute(view_out, axis_name=ax_name, perm=next_value(1 << w))  185 us
    all_to_all x1, waiting for transfers between devices, body(): lax.all_to_all(send_right, 'own', split_axis=0, concat_axis=0, tiled=True)  90.1 us
    all_to_all x1, waiting for transfers between devices, body(): lax.all_to_all(refreshed, 'own', split_axis=0, concat_axis=0, tiled=True)  90 us
    all_to_all x1, waiting for transfers between devices, body(): lax.all_to_all(send_left, 'own', split_axis=0, concat_axis=0, tiled=True)  50.7 us
    all_gather x1, waiting for transfers between devices, body(): old_tables = lax.all_gather(core, 'grp', axis=0, tiled=True)  34.6 us
    all_to_all x1, starting transfers between devices, body(): lax.all_to_all(send_fill, 'own', split_axis=0, concat_axis=0, tiled=True)  18.5 us
  transfers between devices with their start and end apart: 10, of which 10 were waited for; matrix products, arithmetic and copies ran while one was open for 4% of the time, Pallas kernels for 0%

profile of v1, /device:TPU:7, one launch (start us, length us, event | category | flops | bytes accessed | tf_op | source)
XLA Modules:
  0.0 636.9 jit_solution(6885791596796367718)
XLA Ops:
  12.0 18.5 %all-to-all-start.1 = ((s32[64,2,1]{1,2,0:T(1,128)}), s32[64,2,1]{1,2,0:T(1,128)S(1)}, u32[]{:S(2)}, u32[]{:S(2)}) async-start(s32[64,2,1]{1,2,0:T(1,128)} %bitcast.4), calls=%async_computation.1 | async-start | bytes 65536 | tf_op jit(solution)/shard_map/all_to_all | solution.py:59
  31.2 12.7 %all-to-all-done.1 = s32[64,2,1]{1,2,0:T(1,128)S(1)} async-done(((s32[64,2,1]{1,2,0:T(1,128)}), s32[64,2,1]{1,2,0:T(1,128)S(1)}, u32[]{:S(2)}, u32[]{:S(2)}) %all-to-all-start.1) | async-done | bytes 544 | tf_op jit(solution)/shard_map/all_to_all | solution.py:59
  43.8 4.6 all-to-all-start
  50.6 11.3 %all-to-all-done = s32[64,2,1]{1,2,0:T(1,128)S(1)} async-done(((s32[64,2,1]{1,2,0:T(1,128)}), s32[64,2,1]{1,2,0:T(1,128)S(1)}, u32[]{:S(2)}, u32[]{:S(2)}) %all-to-all-start) | async-done | bytes 544 | tf_op jit(solution)/shard_map/all_to_all | solution.py:58
  61.9 4.7 all-to-all-start.3
  70.0 90.1 %all-to-all-done.3 = bf16[128,128,64]{1,2,0:T(8,128)(2,1)S(1)} async-done(((bf16[128,128,64]{1,2,0:T(8,128)(2,1)}), bf16[128,128,64]{1,2,0:T(8,128)(2,1)S(1)}, u32[]{:S(2)}, u32[]{:S(2)}) %all-to-all-start.3) | async-done | bytes 2097184 | tf_op jit(solution)/shard_map/all_to_all | solution.py:56
  161.5 10.7 %all-to-all-start.2 = ((bf16[128,128,64]{1,2,0:T(8,128)(2,1)}), bf16[128,128,64]{1,2,0:T(8,128)(2,1)S(1)}, u32[]{:S(2)}, u32[]{:S(2)}) async-start(bf16[128,128,64]{1,2,0:T(8,128)(2,1)} %gather_fusion.2), calls=%async_computation.2 | async-start | bytes 4194304 | tf_op jit(solution)/shard_map/all_to_all | solution.py:55
  176.7 34.6 %all-gather.2.cloned.1.call-done = bf16[160,64,64]{2,1,0:T(8,128)(2,1)} async-done(((bf16[20,64,64]{2,1,0:T(8,128)(2,1)}), bf16[160,64,64]{2,1,0:T(8,128)(2,1)}) %all-gather.2.cloned.1.call-update) | async-done | bytes 1310736 | tf_op jit(solution)/shard_map/all_gather | solution.py:49
  211.3 3.9 gather_fusion.3
  215.2 50.7 %all-to-all-done.2 = bf16[128,128,64]{1,2,0:T(8,128)(2,1)S(1)} async-done(((bf16[128,128,64]{1,2,0:T(8,128)(2,1)}), bf16[128,128,64]{1,2,0:T(8,128)(2,1)S(1)}, u32[]{:S(2)}, u32[]{:S(2)}) %all-to-all-start.2) | async-done | bytes 2097184 | tf_op jit(solution)/shard_map/all_to_all | solution.py:55
  265.9 11.2 %all-to-all-start.4 = ((bf16[64,2,128]{2,1,0:T(2,128)(2,1)}), bf16[64,2,128]{2,1,0:T(2,128)(2,1)S(1)}, u32[]{:S(2)}, u32[]{:S(2)}) async-start(bf16[64,2,128]{2,1,0:T(2,128)(2,1)} %bitcast.6), calls=%async_computation.4 | async-start | bytes 65536 | tf_op jit(solution)/shard_map/all_to_all | solution.py:57
  280.3 10.0 %all-to-all-done.4 = bf16[64,2,128]{2,1,0:T(2,128)(2,1)S(1)} async-done(((bf16[64,2,128]{2,1,0:T(2,128)(2,1)}), bf16[64,2,128]{2,1,0:T(2,128)(2,1)S(1)}, u32[]{:S(2)}, u32[]{:S(2)}) %all-to-all-start.4) | async-done | bytes 32800 | tf_op jit(solution)/shard_map/all_to_all | solution.py:57
  290.4 4.8 fusion
  295.2 4.8 copy.30
  303.5 5.4 collective-permute-start
  308.9 6.8 %collective-permute-done = f32[160,64,64]{0,2,1:T(8,128)S(1)} collective-permute-done((f32[160,64,64]{0,2,1:T(8,128)S(1)}, f32[160,64,64]{0,2,1:T(8,128)S(1)}, u32[]{:S(2)}, u32[]{:S(2)}) %collective-permute-start) | collective-permute-done | bytes 2621472 | tf_op jit(solution)/shard_map/ppermute | solution.py:13
  319.2 91.2 %collective-permute-done.1 = f32[160,64,64]{0,2,1:T(8,128)S(1)} collective-permute-done((f32[160,64,64]{0,2,1:T(8,128)S(1)}, f32[160,64,64]{0,2,1:T(8,128)S(1)}, u32[]{:S(2)}, u32[]{:S(2)}) %collective-permute-start.1) | collective-permute-done | bytes 2621472 | tf_op jit(solution)/shard_map/ppermute | solution.py:13
  416.2 4.9 copy.26
  421.2 86.7 %collective-permute-done.2 = f32[160,64,64]{0,2,1:T(8,128)} collective-permute-done((f32[160,64,64]{0,2,1:T(8,128)}, f32[160,64,64]{0,2,1:T(8,128)}, u32[]{:S(2)}, u32[]{:S(2)}) %collective-permute-start.2) | collective-permute-done | bytes 2621472 | tf_op jit(solution)/shard_map/ppermute | solution.py:13
  507.8 6.6 %subtract_convert_fusion = bf16[160,64,64]{0,2,1:T(8,128)(2,1)} fusion(f32[160,64,64]{0,2,1:T(8,128)} %add.68, f32[160,64,64]{0,2,1:T(8,128)} %collective-permute-done.2, bf16[160,64,64]{0,2,1:T(8,128)(2,1)} %copy.26), kind=kLoop, calls=%fused_computation.8 | loop fusion | flops 2621440 | bytes 7864320 | tf_op jit(solution)/shard_map/convert_element_type | solution.py:70
  514.4 5.0 copy.31
  519.4 3.9 gather_fusion.6
  527.1 5.7 all-to-all-start.5
  536.8 90.0 %all-to-all-done.5 = bf16[128,128,64]{1,2,0:T(8,128)(2,1)} async-done(((bf16[128,128,64]{1,2,0:T(8,128)(2,1)}), bf16[128,128,64]{1,2,0:T(8,128)(2,1)}, u32[]{:S(2)}, u32[]{:S(2)}) %all-to-all-start.5) | async-done | bytes 2097184 | tf_op jit(solution)/shard_map/all_to_all | solution.py:77
  (46 shorter events, 44.1 us)
Async XLA Ops:
  7.2 41.3 %copy-start = (bf16[64,128,64]{1,2,0:T(8,128)(2,1)S(1)}, bf16[64,128,64]{1,2,0:T(8,128)(2,1)}, u32[]{:S(2)}) copy-start(bf16[64,128,64]{1,2,0:T(8,128)(2,1)} %param.7) | copy-start | bytes 3145732
  12.0 31.9 %all-to-all-start.1 = ((s32[64,2,1]{1,2,0:T(1,128)}), s32[64,2,1]{1,2,0:T(1,128)S(1)}, u32[]{:S(2)}, u32[]{:S(2)}) async-start(s32[64,2,1]{1,2,0:T(1,128)} %bitcast.4), calls=%async_computation.1 | async-start | bytes 65536 | tf_op jit(solution)/shard_map/all_to_all | solution.py:59
  43.8 18.1 %all-to-all-start = ((s32[64,2,1]{1,2,0:T(1,128)}), s32[64,2,1]{1,2,0:T(1,128)S(1)}, u32[]{:S(2)}, u32[]{:S(2)}) async-start(s32[64,2,1]{1,2,0:T(1,128)} %bitcast.2), calls=%async_computation | async-start | bytes 65536 | tf_op jit(solution)/shard_map/all_to_all | solution.py:58
  61.9 98.2 %all-to-all-start.3 = ((bf16[128,128,64]{1,2,0:T(8,128)(2,1)}), bf16[128,128,64]{1,2,0:T(8,128)(2,1)S(1)}, u32[]{:S(2)}, u32[]{:S(2)}) async-start(bf16[128,128,64]{1,2,0:T(8,128)(2,1)} %gather_fusion.4), calls=%async_computation.3 | async-start | bytes 4194304 | tf_op jit(solution)/shard_map/all_to_all | solution.py:56
  70.0 102.9 %copy-start.3 = (bf16[64,128]{1,0:T(8,128)(2,1)S(1)}, bf16[64,128]{1,0:T(8,128)(2,1)}, u32[]{:S(2)}) copy-start(bf16[64,128]{1,0:T(8,128)(2,1)} %param.8) | copy-start | bytes 49156
  160.2 1.3 copy-start.1
  161.5 104.4 %all-to-all-start.2 = ((bf16[128,128,64]{1,2,0:T(8,128)(2,1)}), bf16[128,128,64]{1,2,0:T(8,128)(2,1)S(1)}, u32[]{:S(2)}, u32[]{:S(2)}) async-start(bf16[128,128,64]{1,2,0:T(8,128)(2,1)} %gather_fusion.2), calls=%async_computation.2 | async-start | bytes 4194304 | tf_op jit(solution)/shard_map/all_to_all | solution.py:55
  172.2 39.1 %all-gather.2.cloned.1.call-start = ((), (), s32[]{:S(2)}) async-start(), calls=%async_computation.6 | async-start | bytes 2949120 | tf_op jit(solution)/shard_map/all_gather | solution.py:49
  265.9 24.4 %all-to-all-start.4 = ((bf16[64,2,128]{2,1,0:T(2,128)(2,1)}), bf16[64,2,128]{2,1,0:T(2,128)(2,1)S(1)}, u32[]{:S(2)}, u32[]{:S(2)}) async-start(bf16[64,2,128]{2,1,0:T(2,128)(2,1)} %bitcast.6), calls=%async_computation.4 | async-start | bytes 65536 | tf_op jit(solution)/shard_map/all_to_all | solution.py:57
  303.5 12.2 %collective-permute-start = (f32[160,64,64]{0,2,1:T(8,128)S(1)}, f32[160,64,64]{0,2,1:T(8,128)S(1)}, u32[]{:S(2)}, u32[]{:S(2)}) collective-permute-start(f32[160,64,64]{0,2,1:T(8,128)S(1)} %fusion.1), channel_id=1, source_target_pairs={{0,64},{64,0},{128,192},{192,128},{256,320},{320,256},{384,448},{4... | collective-permute-start | bytes 7864328 | tf_op jit(solution)/shard_map/ppermute | solution.py:13
  316.7 93.7 %collective-permute-start.1 = (f32[160,64,64]{0,2,1:T(8,128)S(1)}, f32[160,64,64]{0,2,1:T(8,128)S(1)}, u32[]{:S(2)}, u32[]{:S(2)}) collective-permute-start(f32[160,64,64]{0,2,1:T(8,128)S(1)} %add.67), channel_id=1, source_target_pairs={{0,128},{64,192},{128,0},{192,64},{256,384},{320,448},{384,256},{4... | collective-permute-start | bytes 7864328 | tf_op jit(solution)/shard_map/ppermute | solution.py:13
  413.2 94.6 %collective-permute-start.2 = (f32[160,64,64]{0,2,1:T(8,128)}, f32[160,64,64]{0,2,1:T(8,128)}, u32[]{:S(2)}, u32[]{:S(2)}) collective-permute-start(f32[160,64,64]{0,2,1:T(8,128)} %add.68), channel_id=1, source_target_pairs={{0,256},{64,320},{128,384},{192,448},{256,0},{320,64},{384,128},{4... | collective-permute-start | bytes 7864328 | tf_op jit(solution)/shard_map/ppermute | solution.py:13
  527.1 5.7 copy-start.2
  527.1 99.7 %all-to-all-start.5 = ((bf16[128,128,64]{1,2,0:T(8,128)(2,1)}), bf16[128,128,64]{1,2,0:T(8,128)(2,1)}, u32[]{:S(2)}, u32[]{:S(2)}) async-start(bf16[128,128,64]{1,2,0:T(8,128)(2,1)} %convolution_convert_fusion), calls=%async_computation.5 | async-start | bytes 4194304 | tf_op jit(solution)/shard_map/all_to_all | solution.py:77
Sparse Core Ops, SparseCore 0:
  175.1 36.1 all-gather.1
